TPU v7x, 32 devices: a whole 2x2x4 slice. The times are simulated.
32 devices in a mesh: ctx: 8 (over z, y), fsdp: 4 (over x, core).
Axes of the slice: x: 2, y: 2, z: 4, core: 2. Of those that a mesh axis runs over, the one named last changes fastest.
Arguments:
- tokens: bfloat16 [2048, 4096], P('ctx', 'fsdp'), may hold values from -150 to 150
- norm_gain: float32 [4096], replicated, may hold values from 0.1 to 1.9
- in_weight: bfloat16 [4096, 3, 4096], P('ctx', None, 'fsdp'), may hold values from -0.09375 to 0.09375
- short_filter: float32 [3, 3, 4096], P(None, None, 'fsdp'), may hold values from -3.5 to 3.5
- long_filter: bfloat16 [256, 128], P('fsdp'), may hold values from -0.5 to 0.5
- skip_gain: float32 [4096], P('fsdp'), may hold values from -4 to 4
- out_weight: bfloat16 [4096, 4096], P('fsdp', 'ctx'), may hold values from -0.09375 to 0.09375
Outputs:
- mixed: bfloat16 [2048, 4096], P('ctx', 'fsdp')
All inputs are finite; a program needn't handle non-finite values.
Results may differ from a plain program's by a relative error of at most 0.0091.
Values may be sent and summed in bfloat16 or wider, within the bound.
A program may use at most 128 MiB of HBM per device.

v0:
```python
import jax
import jax.numpy as jnp
from jax import lax
from jax.sharding import PartitionSpec as P


def passed_along(block, axis, distance):
    devices = range(lax.axis_size(axis))
    route = [(i - distance, i) for i in devices if i - distance in devices]
    return lax.ppermute(block, axis, route)


def toeplitz_blocks(long_filter, row_count):
    groups = long_filter.shape[0]
    flen = long_filter.shape[1]
    window = flen + row_count - 1
    reversed_taps = long_filter[:, ::-1]
    padded = jnp.concatenate(
        [reversed_taps, jnp.zeros((groups, row_count), long_filter.dtype)], axis=1
    )
    tiled = jnp.tile(padded, (1, row_count))
    return tiled[:, : row_count * window].reshape(groups, row_count, window)


def short_conv(taps, extended):
    return taps[0] * extended[2:] + taps[1] * extended[1:-1] + taps[2] * extended[:-2]


def on_device(tokens, norm_gain, in_weight, short_filter, long_filter, skip_gain, out_weight):
    whole = lax.all_gather(tokens, "fsdp", axis=1, tiled=True)
    row_count = whole.shape[0]
    values = whole.astype(jnp.float32)
    mean_square = jnp.mean(values * values, axis=-1, keepdims=True)
    normed = (values * lax.rsqrt(mean_square + 1e-06) * norm_gain).astype(jnp.bfloat16)
    share = in_weight.shape[2]
    width_all = 3 * share
    weight_rows = lax.all_gather(in_weight, "ctx", axis=0, tiled=True)
    flat_rows = weight_rows.reshape(weight_rows.shape[0], width_all)
    proj = jnp.dot(normed, flat_rows, preferred_element_type=jnp.float32).astype(jnp.bfloat16)
    taps = short_filter.reshape(3, width_all)
    flen = long_filter.shape[1]
    earlier = passed_along(proj[row_count - 2 :], "ctx", 1)
    extended = jnp.concatenate([earlier, proj], axis=0).astype(jnp.float32)
    filtered = short_conv(taps, extended)
    out_gate = filtered[:, :share]
    product = (filtered[:, share : 2 * share] * filtered[:, 2 * share :]).astype(jnp.bfloat16)
    previous = passed_along(product[row_count - (flen - 1) :], "ctx", 1)
    product_ext = jnp.concatenate([previous, product], axis=0)
    groups = long_filter.shape[0]
    group_width = share // groups
    window = row_count + flen - 1
    blocks = toeplitz_blocks(long_filter, row_count)
    conv = jnp.einsum(
        "gts,sgc->tgc",
        blocks,
        product_ext.reshape(window, groups, group_width),
        preferred_element_type=jnp.float32,
    ).reshape(row_count, share)
    gated = (out_gate * (conv + skip_gain * product.astype(jnp.float32))).astype(jnp.bfloat16)
    terms = jnp.dot(
        gated,
        lax.all_gather(out_weight, "ctx", axis=1, tiled=True),
        preferred_element_type=jnp.float32,
    )
    mixed = lax.psum_scatter(terms, "fsdp", scatter_dimension=1, tiled=True).astype(jnp.bfloat16)
    return mixed


def solution(mesh):
    in_specs = (
        P("ctx", "fsdp"),
        P(),
        P("ctx", None, "fsdp"),
        P(None, None, "fsdp"),
        P("fsdp", None),
        P("fsdp"),
        P("fsdp", "ctx"),
    )
    out_specs = P("ctx", "fsdp")
    return jax.shard_map(
        on_device, mesh=mesh, in_specs=in_specs, out_specs=out_specs, check_vma=False
    )
```

profile of v0, /device:TPU:10, one launch (start us, length us, event | category | flops | bytes accessed | tf_op | source)
XLA Modules:
  0.0 706.4 jit_solution(7502111385627137114)
XLA Ops:
  6.5 0.0 all-gather.4.cloned.1.call-start
  6.5 0.7 all-gather.4.cloned.1.call-update
  7.3 0.0 all-gather.6.cloned.1.call-start
  7.3 4.7 copy.10
  12.0 0.0 copy-start.4
  12.0 0.0 all-gather.6.cloned.1.call-update
  12.0 0.0 all-gather.8.cloned.1.call-start
  12.0 0.7 all-gather.8.cloned.1.call-update
  12.7 0.0 reduce-scatter.2.cloned.1.call-start
  12.8 18.9 %all-gather.4.cloned.1.call-done = bf16[256,4096]{1,0:T(8,128)(2,1)} async-done(((bf16[256,1024]{1,0:T(8,128)(2,1)}), bf16[256,4096]{1,0:T(8,128)(2,1)}) %all-gather.4.cloned.1.call-update) | async-done | bytes 2097168 | tf_op jit(solution)/shard_map/all_gather | solution.py:30
  31.7 2.1 fusion
  33.8 480.7 %all-gather.6.cloned.1.call-done = bf16[4096,3,1024]{0,2,1:T(8,128)(2,1)} async-done(((bf16[512,3,1024]{0,2,1:T(8,128)(2,1)}), bf16[4096,3,1024]{0,2,1:T(8,128)(2,1)}) %all-gather.6.cloned.1.call-update) | async-done | bytes 25165840 | tf_op jit(solution)/shard_map/all_gather | solution.py:37
  514.5 0.0 copy-done.4
  514.5 0.0 copy-start.2
  514.5 12.2 %convolution_convert_fusion = bf16[256,3072]{1,0:T(8,128)(2,1)S(1)} fusion(bf16[4096,3072]{0,1:T(8,128)(2,1)} %bitcast.15, bf16[256,4096]{1,0:T(8,128)(2,1)} %all-gather.4.cloned.1.call-done, f32[4096]{0:T(1024)S(1)} %copy-done.4, f32[256]{0:T(256)S(1)} %add_rsqrt_fusion), kind=kOutput, calls=%fused_computation.5 | convolution fusion | flops 6447431680 | bytes 28853248 | tf_op jit(solution)/shard_map/dot_general | solution.py:39
  526.8 2.5 collective-permute-start
  529.4 0.0 copy-done.2
  529.4 4.3 collective-permute-done
  533.7 0.5 maximum_convert_fusion
  534.2 0.9 fusion.3
  535.1 0.0 copy-start.3
  535.1 0.1 fusion.8
  535.2 0.0 copy-start
  535.2 0.8 copy-done
  536.0 0.1 slice.58
  536.1 2.1 collective-permute-start.1
  538.2 0.0 copy-done.3
  538.2 0.1 rev.3
  538.3 5.6 tile.4
  543.9 11.6 %copy.13 = bf16[8,8,256,384]{3,1,2,0:T(8,128)(2,1)S(1)} copy(bf16[8,8,256,384]{3,2,1,0:T(8,128)(2,1)} %bitcast.11) | data formatting | bytes 25165824
  555.6 5.2 slice.59
  560.8 34.2 %reshape.35 = bf16[64,256,383]{2,1,0:T(8,128)(2,1)} reshape(bf16[64,98048]{1,0:T(8,128)(2,1)} %slice.59) | data formatting | bytes 25100288 | tf_op jit(solution)/shard_map/reshape | solution.py:22
  595.0 0.0 collective-permute-done.1
  595.0 2.2 pad_maximum_fusion
  597.2 2.3 copy.11
  599.5 0.0 copy-start.1
  599.5 9.4 %fusion.14 = f32[64,16,256]{2,1,0:T(8,128)} fusion(bf16[383,64,16]{0,2,1:T(8,128)(2,1)} %bitcast.14, bf16[64,256,383]{2,1,0:T(8,128)(2,1)} %reshape.35), kind=kOutput, calls=%fused_computation.23 | convolution fusion | flops 200802304 | bytes 14383104 | tf_op jit(solution)/shard_map/gts,sgc->tgc/dot_general | solution.py:53
  608.9 2.5 copy.12
  611.4 34.4 %all-gather.8.cloned.1.call-done = bf16[1024,4096]{1,0:T(8,128)(2,1)} async-done(((bf16[1024,512]{1,0:T(8,128)(2,1)}), bf16[1024,4096]{1,0:T(8,128)(2,1)}) %all-gather.8.cloned.1.call-update) | async-done | bytes 8388624 | tf_op jit(solution)/shard_map/all_gather | solution.py:62
  645.9 0.0 copy-done.1
  645.9 8.2 %fusion.10 = f32[256,4096]{1,0:T(8,128)} fusion(bf16[1024,4096]{1,0:T(8,128)(2,1)} %all-gather.8.cloned.1.call-done, f32[256,3072]{1,0:T(8,128)S(1)} %fusion.3, f32[256,1024]{1,0:T(8,128)} %copy.12, bf16[256,1024]{1,0:T(8,128)(2,1)} %copy-done, f32[1024]{0:T(1024)S(1)} %copy-done.1), kind=kOutput, calls=%fused_computation.19 | convolution fusion | flops 2148794368 | bytes 15208448 | tf_op jit(solution)/shard_map/dot_general | solution.py:60
  654.0 0.0 reduce-scatter.2.cloned.1.call-update
  654.1 43.7 %reduce-scatter.2.cloned.1.call-done = f32[256,1024]{1,0:T(8,128)} async-done(((f32[256,4096]{1,0:T(8,128)}), f32[256,1024]{1,0:T(8,128)}) %reduce-scatter.2.cloned.1.call-update) | async-done | bytes 1048592 | tf_op jit(solution)/shard_map/reduce_scatter | solution.py:65
  697.7 2.1 convert_element_type.31
  (7 shorter events, 0.1 us)
Async XLA Ops:
  6.5 25.2 %all-gather.4.cloned.1.call-start = ((), (), s32[]{:S(2)}) async-start(), calls=%async_computation.1 | async-start | bytes 2621440 | tf_op jit(solution)/shard_map/all_gather | solution.py:30
  7.3 507.3 %all-gather.6.cloned.1.call-start = ((), (), s32[]{:S(2)}) async-start(), calls=%async_computation.2 | async-start | bytes 28311552 | tf_op jit(solution)/shard_map/all_gather | solution.py:37
  12.0 502.6 %copy-start.4 = (f32[4096]{0:T(1024)S(1)}, f32[4096]{0:T(1024)}, u32[]{:S(2)}) copy-start(f32[4096]{0:T(1024)} %param.8) | copy-start | bytes 49156
  12.0 633.9 %all-gather.8.cloned.1.call-start = ((), (), s32[]{:S(2)}) async-start(), calls=%async_computation.3 | async-start | bytes 9437184 | tf_op jit(solution)/shard_map/all_gather | solution.py:62
  12.7 685.0 %reduce-scatter.2.cloned.1.call-start = ((), (), s32[]{:S(2)}) async-start(), calls=%async_computation.4 | async-start | bytes 5242880 | tf_op jit(solution)/shard_map/reduce_scatter | solution.py:65
  514.5 14.8 %copy-start.2 = (f32[3,3,1024]{2,1,0:T(4,128)S(1)}, f32[3,3,1024]{2,1,0:T(4,128)}, u32[]{:S(2)}) copy-start(f32[3,3,1024]{2,1,0:T(4,128)} %param.10) | copy-start | bytes 110596
  526.8 6.9 collective-permute-start
  535.1 3.1 copy-start.3
  535.2 0.8 copy-start
  536.1 58.9 %collective-permute-start.1 = (bf16[127,1024]{1,0:T(8,128)(2,1)S(1)}, bf16[127,1024]{1,0:T(8,128)(2,1)}, u32[]{:S(2)}, u32[]{:S(2)}) collective-permute-start(bf16[127,1024]{1,0:T(8,128)(2,1)S(1)} %slice.58), channel_id=1, source_target_pairs={{0,4},{4,8},{8,12},{12,16},{16,20},{20,24},{24,28},{1,5},{5,9},{9,... | collective-permute-start | bytes 780296 | tf_op jit(solution)/shard_map/ppermute | solution.py:10
  599.5 46.3 %copy-start.1 = (f32[1024]{0:T(1024)S(1)}, f32[1024]{0:T(1024)}, u32[]{:S(2)}) copy-start(f32[1024]{0:T(1024)} %param.12) | copy-start | bytes 12292
Sparse Core Ops, SparseCore 0:
  8.9 22.7 all-gather.3
  33.2 481.2 all-gather.5
  516.6 129.2 all-gather.7
  654.2 43.5 reduce-scatter.1
where the time goes:
time: 709 us; the launch traced here: 706 us
  waiting for transfers between devices  583 us (82%)
  local copies, waits for them, and re-layouts  67.2 us (9%)
  matrix products  29.8 us (4%)
  between operations  13.3 us (2%)
  other arithmetic  7.9 us (1%)
    all_gather x1, waiting for transfers between devices, on_device(): weight_rows = lax.all_gather(in_weight, 'ctx', axis=0, tiled=True)  481 us
    reduce_scatter x1, waiting for transfers between devices, on_device(): lax.psum_scatter(terms, 'fsdp', scatter_dimension=1, tiled=True)  43.7 us
    all_gather x1, waiting for transfers between devices, on_device(): lax.all_gather(out_weight, 'ctx', axis=1, tiled=True)  34.4 us
    reshape x1, local copies, waits for them, and re-layouts, toeplitz_blocks(): return tiled[:, :row_count * window].reshape(groups, row_count, window)  34.2 us
    all_gather x1, waiting for transfers between devices, on_device(): whole = lax.all_gather(tokens, 'fsdp', axis=1, tiled=True)  18.9 us
    unnamed x12, local copies, waits for them, and re-layouts  17.1 us
  transfers between devices with their start and end apart: 6, of which 5 were waited for; matrix products, arithmetic and copies ran while one was open for 13% of the time, Pallas kernels for 0%

commit v1 on v0

--- a/solution.py
+++ b/solution.py
@@ -1,6 +1,10 @@
+import functools
+
 import jax
 import jax.numpy as jnp
 from jax import lax
+from jax.experimental import pallas as pl
+from jax.experimental.pallas import tpu as pltpu
 from jax.sharding import PartitionSpec as P
 
 
@@ -26,7 +30,7 @@
     return taps[0] * extended[2:] + taps[1] * extended[1:-1] + taps[2] * extended[:-2]
 
 
-def on_device(tokens, norm_gain, in_weight, short_filter, long_filter, skip_gain, out_weight):
+def slab_plan(tokens, norm_gain, in_weight, short_filter, long_filter, skip_gain, out_weight):
     whole = lax.all_gather(tokens, "fsdp", axis=1, tiled=True)
     row_count = whole.shape[0]
     values = whole.astype(jnp.float32)
@@ -66,6 +70,360 @@
     return mixed
 
 
+MESH = pl.DeviceIdType.MESH
+LANE = 128
+
+
+def meet(peers):
+    barrier = pltpu.get_barrier_semaphore()
+    for peer in peers:
+        pl.semaphore_signal(barrier, inc=1, device_id=peer, device_id_type=MESH)
+    pl.semaphore_wait(barrier, len(peers))
+
+
+class Relay:
+    def __init__(self, own, place, sends, recvs, across):
+        self.me = (lax.axis_index("ctx"), lax.axis_index("fsdp"))
+        self.line = lax.axis_size("ctx") // 2
+        self.width = lax.axis_size("fsdp")
+        self.high, self.low = self.me[0] // 2, self.me[0] % 2
+        self.own, self.place = own, place
+        self.sends, self.recvs = sends, recvs
+        self.across = across
+
+    def copy(self, kind, block, target, own=False):
+        index = block[0] * self.width + block[1]
+        return pltpu.make_async_remote_copy(
+            src_ref=self.own if own else self.place(*block),
+            dst_ref=self.place(*block),
+            send_sem=self.sends.at[kind, index],
+            recv_sem=self.recvs.at[index],
+            device_id=target,
+            device_id_type=MESH,
+        )
+
+    def visit(self, kind, block, own, action):
+        ctx, fsdp = self.me
+        if kind == 0:
+            @pl.when(self.high < self.line - 1)
+            def _():
+                action(self.copy(0, block, (ctx + 2, fsdp), own))
+        elif kind == 1:
+            @pl.when(self.high > 0)
+            def _():
+                action(self.copy(1, block, (ctx - 2, fsdp), own))
+        elif kind == 2:
+            action(self.copy(2, block, (ctx + 1 - 2 * self.low, fsdp), own))
+        elif kind == 3:
+            x, core = fsdp // 2, fsdp % 2
+            action(self.copy(3, block, (ctx, (1 - x) * 2 + core), own))
+        else:
+            action(self.copy(4, block, (ctx, fsdp + 1 - 2 * (fsdp % 2)), own))
+
+    def arrive(self, block):
+        self.copy(0, block, (self.me[0], self.me[1])).wait_recv()
+
+    def run(self, action, landed, after_first=None):
+        ctx, fsdp = self.me
+        high, low = self.high, self.low
+        for kind in (0, 1, 2) + self.across:
+            self.visit(kind, (ctx, fsdp), True, action)
+        for away in range(self.line + 1):
+            if 1 <= away < self.line:
+                @pl.when(high >= away)
+                def _():
+                    block = ((high - away) * 2 + low, fsdp)
+                    landed(block)
+                    for kind in (0, 2) + self.across:
+                        self.visit(kind, block, False, action)
+
+                @pl.when(high + away < self.line)
+                def _():
+                    block = ((high + away) * 2 + low, fsdp)
+                    landed(block)
+                    for kind in (1, 2) + self.across:
+                        self.visit(kind, block, False, action)
+            if away == 1 and after_first is not None:
+                after_first()
+            if away >= 1:
+                back = away - 1
+                for sign in (-1, 1) if back else (1,):
+                    at = high + sign * back
+
+                    @pl.when((at >= 0) & (at < self.line))
+                    def _():
+                        block = (at * 2 + 1 - low, fsdp)
+                        landed(block)
+                        for kind in self.across:
+                            self.visit(kind, block, False, action)
+        if 3 in self.across:
+            other = (1 - fsdp // 2) * 2 + fsdp % 2
+            for step in range(2 * self.line):
+                block = ((ctx + step) % (2 * self.line), other)
+                landed(block)
+                self.visit(4, block, False, action)
+            for step in range(2 * self.line):
+                for x in range(2):
+                    landed(((ctx + step) % (2 * self.line), x * 2 + 1 - fsdp % 2))
+
+    def go(self, after_first=None):
+        self.run(lambda copy: copy.start(), self.arrive, after_first)
+
+    def finish(self):
+        self.run(lambda copy: copy.wait_send(), lambda block: None)
+
+
+def spread_kernel(rows_ref, weight_ref, all_ref, mine_ref, sends, recvs, w_sends, w_recvs, local):
+    ctx, fsdp = lax.axis_index("ctx"), lax.axis_index("fsdp")
+    slabs = lax.axis_size("ctx")
+    rows, features = rows_ref.shape
+    others = [((ctx + step) % slabs, fsdp) for step in range(1, slabs)]
+    x, core = fsdp // 2, fsdp % 2
+    meet(others + [(ctx, (1 - x) * 2 + core), (ctx, x * 2 + 1 - core)])
+
+    def place(slab, part):
+        return all_ref.at[pl.ds(slab * rows, rows), pl.ds(part * features, features)]
+
+    own = [
+        pltpu.make_async_copy(rows_ref, place(ctx, fsdp), local.at[0]),
+        pltpu.make_async_copy(weight_ref.at[ctx], mine_ref.at[ctx], local.at[1]),
+    ]
+
+    def weight_copy(step):
+        target = (ctx + step) % slabs
+        return pltpu.make_async_remote_copy(
+            src_ref=weight_ref.at[target],
+            dst_ref=mine_ref.at[ctx],
+            send_sem=w_sends.at[step],
+            recv_sem=w_recvs.at[step],
+            device_id=(target, fsdp),
+            device_id_type=MESH,
+        )
+
+    def send_weights():
+        for step in range(1, slabs):
+            weight_copy(step).start()
+
+    relay = Relay(rows_ref, place, sends, recvs, (3, 4))
+    for copy in own:
+        copy.start()
+    relay.go(send_weights)
+    for step in range(1, slabs):
+        source = (ctx + slabs - step) % slabs
+        pltpu.make_async_remote_copy(
+            src_ref=weight_ref.at[source],
+            dst_ref=mine_ref.at[source],
+            send_sem=w_sends.at[step],
+            recv_sem=w_recvs.at[step],
+            device_id=(source, fsdp),
+            device_id_type=MESH,
+        ).wait_recv()
+    relay.finish()
+    for step in range(1, slabs):
+        weight_copy(step).wait_send()
+    for copy in own:
+        copy.wait()
+
+
+def collect_kernel(cols_ref, all_ref, sends, recvs, local):
+    ctx, fsdp = lax.axis_index("ctx"), lax.axis_index("fsdp")
+    slabs = lax.axis_size("ctx")
+    width = cols_ref.shape[1]
+    meet([((ctx + step) % slabs, fsdp) for step in range(1, slabs)])
+
+    def place(slab, part):
+        return all_ref.at[:, pl.ds(slab * width, width)]
+
+    own = pltpu.make_async_copy(cols_ref, place(ctx, fsdp), local.at[0])
+    own.start()
+    relay = Relay(cols_ref, place, sends, recvs, ())
+    relay.go()
+    relay.finish()
+    own.wait()
+
+
+def deliver_kernel(terms_ref, out_ref, sends, recvs, local):
+    ctx, fsdp = lax.axis_index("ctx"), lax.axis_index("fsdp")
+    slabs, parts = lax.axis_size("ctx"), lax.axis_size("fsdp")
+    fold = slabs // parts
+    width = terms_ref.shape[2]
+    home = ctx // fold
+    mixed_in = home == fsdp
+
+    barrier = pltpu.get_barrier_semaphore()
+    for slab in range(slabs):
+        @pl.when(jnp.logical_not(mixed_in & (slab == ctx)))
+        def _():
+            pl.semaphore_signal(barrier, inc=1, device_id=(slab, home), device_id_type=MESH)
+
+    for part in range(parts):
+        for half in range(fold):
+            source = fsdp * fold + half
+
+            @pl.when(jnp.logical_not((part == fsdp) & (source == ctx)))
+            def _():
+                pl.semaphore_signal(barrier, inc=1, device_id=(source, part), device_id_type=MESH)
+
+    @pl.when(mixed_in)
+    def _():
+        pl.semaphore_wait(barrier, slabs + parts * fold - 2)
+
+    @pl.when(jnp.logical_not(mixed_in))
+    def _():
+        pl.semaphore_wait(barrier, slabs + parts * fold)
+
+    def slot(part, source):
+        return out_ref.at[part, :, pl.ds((source % fold) * width, width)]
+
+    def outgoing(slab):
+        return pltpu.make_async_remote_copy(
+            src_ref=terms_ref.at[slab],
+            dst_ref=slot(fsdp, ctx),
+            send_sem=sends.at[slab],
+            recv_sem=recvs.at[fsdp * fold + ctx % fold],
+            device_id=(slab, home),
+            device_id_type=MESH,
+        )
+
+    def each(action):
+        for step in range(slabs):
+            slab = (ctx + step) % slabs
+
+            @pl.when(jnp.logical_not(mixed_in & (slab == ctx)))
+            def _():
+                action(slab)
+
+    own = pltpu.make_async_copy(terms_ref.at[ctx], slot(fsdp, ctx), local.at[0])
+    each(lambda slab: outgoing(slab).start())
+
+    @pl.when(mixed_in)
+    def _():
+        own.start()
+
+    for part in range(parts):
+        for half in range(fold):
+            source = fsdp * fold + half
+
+            @pl.when(jnp.logical_not((part == fsdp) & (source == ctx)))
+            def _():
+                pltpu.make_async_remote_copy(
+                    src_ref=terms_ref.at[0],
+                    dst_ref=slot(part, source),
+                    send_sem=sends.at[0],
+                    recv_sem=recvs.at[part * fold + half],
+                    device_id=(source, part),
+                    device_id_type=MESH,
+                ).wait_recv()
+
+    each(lambda slab: outgoing(slab).wait_send())
+
+    @pl.when(mixed_in)
+    def _():
+        own.wait()
+
+
+VMEM_SPEC = pl.BlockSpec(memory_space=pltpu.VMEM)
+ANY_SPEC = pl.BlockSpec(memory_space=pl.ANY)
+DMA = pltpu.SemaphoreType.DMA
+
+
+def params(number):
+    return pltpu.CompilerParams(collective_id=number, has_side_effects=True)
+
+
+def spread(rows, weights):
+    slabs, parts = lax.axis_size("ctx"), lax.axis_size("fsdp")
+    return pl.pallas_call(
+        spread_kernel,
+        out_shape=(
+            jax.ShapeDtypeStruct((rows.shape[0] * slabs, rows.shape[1] * parts), rows.dtype),
+            jax.ShapeDtypeStruct(weights.shape, weights.dtype),
+        ),
+        in_specs=[VMEM_SPEC, VMEM_SPEC],
+        out_specs=(ANY_SPEC, ANY_SPEC),
+        scratch_shapes=[
+            DMA((5, slabs * parts)), DMA((slabs * parts,)), DMA((slabs,)), DMA((slabs,)), DMA((2,)),
+        ],
+        compiler_params=params(0),
+    )(rows, weights)
+
+
+def collect(cols):
+    slabs, parts = lax.axis_size("ctx"), lax.axis_size("fsdp")
+    return pl.pallas_call(
+        collect_kernel,
+        out_shape=jax.ShapeDtypeStruct((cols.shape[0], cols.shape[1] * slabs), cols.dtype),
+        in_specs=[VMEM_SPEC],
+        out_specs=ANY_SPEC,
+        scratch_shapes=[DMA((3, slabs * parts)), DMA((slabs * parts,)), DMA((1,))],
+        compiler_params=params(1),
+    )(cols)
+
+
+def deliver(terms):
+    slabs, parts = lax.axis_size("ctx"), lax.axis_size("fsdp")
+    fold = slabs // parts
+    return pl.pallas_call(
+        deliver_kernel,
+        out_shape=jax.ShapeDtypeStruct((parts, terms.shape[1], terms.shape[2] * fold), terms.dtype),
+        in_specs=[VMEM_SPEC],
+        out_specs=ANY_SPEC,
+        scratch_shapes=[DMA((slabs,)), DMA((parts * fold,)), DMA((1,))],
+        compiler_params=params(2),
+    )(terms)
+
+
+def channel_plan(tokens, norm_gain, in_weight, short_filter, long_filter, skip_gain, out_weight):
+    ctx, fsdp = lax.axis_index("ctx"), lax.axis_index("fsdp")
+    slabs, parts = lax.axis_size("ctx"), lax.axis_size("fsdp")
+    rows, features = tokens.shape
+    positions = rows * slabs
+    share = in_weight.shape[2]
+    own = share // slabs
+    values = tokens.astype(jnp.float32)
+    mean_square = lax.psum(jnp.sum(values * values, axis=-1, keepdims=True), "fsdp") / (features * parts)
+    gain = lax.dynamic_slice_in_dim(norm_gain, fsdp * features, features, 0)
+    normed = (values * lax.rsqrt(mean_square + 1e-06) * gain).astype(jnp.bfloat16)
+
+    pieces = in_weight.reshape(in_weight.shape[0], 3, slabs, own).transpose(2, 0, 1, 3)
+    pieces = pieces.reshape(slabs, in_weight.shape[0], 3 * own)
+    whole, weights = spread(normed, pieces)
+    weights = weights.reshape(slabs * in_weight.shape[0], 3 * own)
+    proj = jnp.dot(whole, weights, preferred_element_type=jnp.float32).astype(jnp.bfloat16)
+
+    taps = lax.dynamic_slice_in_dim(short_filter, ctx * own, own, 2).reshape(3, 3 * own)
+    extended = jnp.pad(proj.astype(jnp.float32), ((2, 0), (0, 0)))
+    filtered = short_conv(taps, extended)
+    product = (filtered[:, own : 2 * own] * filtered[:, 2 * own :]).astype(jnp.bfloat16)
+
+    flen = long_filter.shape[1]
+    group_count = long_filter.shape[0] // slabs
+    group_width = own // group_count
+    filters = lax.dynamic_slice_in_dim(long_filter, ctx * group_count, group_count, 0)
+    blocks = jnp.pad(toeplitz_blocks(filters, flen), ((0, 0), (0, 0), (1, 0)))
+    count = positions // flen
+    tiles = product.reshape(count, flen, group_count, group_width)
+    before = jnp.pad(tiles, ((1, 0), (0, 0), (0, 0), (0, 0)))[:-1]
+    windows = jnp.concatenate([before, tiles], axis=1)
+    conv = jnp.einsum("gts,bsgc->btgc", blocks, windows, preferred_element_type=jnp.float32)
+    conv = conv.reshape(positions, own)
+    skip = lax.dynamic_slice_in_dim(skip_gain, ctx * own, own, 0)
+    gated = (filtered[:, :own] * (conv + skip * product.astype(jnp.float32))).astype(jnp.bfloat16)
+
+    terms = jnp.dot(collect(gated), out_weight, preferred_element_type=jnp.float32)
+    terms = terms.astype(jnp.bfloat16).reshape(slabs, rows, out_weight.shape[1])
+    arrived = deliver(terms)
+    return jnp.sum(arrived.astype(jnp.float32), axis=0).astype(jnp.bfloat16)
+
+
+def on_device(tokens, *rest):
+    slabs, parts = lax.axis_size("ctx"), lax.axis_size("fsdp")
+    own = rest[1].shape[2] // slabs
+    gathered = tokens.size * slabs * parts * 2
+    fits = parts == 4 and slabs % parts == 0 and own % LANE == 0 and gathered <= 2**25
+    return (channel_plan if fits else slab_plan)(tokens, *rest)
+
+
 def solution(mesh):
     in_specs = (
         P("ctx", "fsdp"),

time: 709 us -> 308 us (0.43)
  waiting for transfers between devices: 583 us -> 0 us
  Pallas kernels: 0 us -> 241 us
  local copies, waits for them, and re-layouts: 67.2 us -> 20.8 us
  between operations: 13.3 us -> 0.13 us
  matrix products: 29.8 us -> 20.8 us
    all_gather x3 -> x0, waiting for transfers between devices: 534 us -> none  [the longest x1 481 us: on_device(): weight_rows = lax.all_gather(in_weight, 'ctx', axis=0, tiled=True)]
    pallas_call x0 -> x3, Pallas kernels: none -> 241 us  [the longest x1 115 us: spread(): pl.pallas_call(spread_kernel, out_shape=(jax.ShapeDtypeStruct((rows.shape...]
    reduce_scatter x1 -> x0, waiting for transfers between devices: 43.7 us -> none  [on_device(): lax.psum_scatter(terms, 'fsdp', scatter_dimension=1, tiled=True)]
    reshape x1, local copies, waits for them, and re-layouts: 34.2 us -> 1.36 us  [toeplitz_blocks(): return tiled[:, :row_count * window].reshape(groups, row_count, window)]
    unnamed x12 -> x7, local copies, waits for them, and re-layouts: 17.1 us -> 6.81 us
    dot_general x3, matrix products: 29.8 us -> 20.8 us  [the longest x1 14.4 us: channel_plan(): jnp.dot(whole, weights, preferred_element_type=jnp.float32)]
  transfers between devices with their start and end apart: 6 -> 0, of which waited for: 5 -> 0; matrix products, arithmetic and copies ran while one was open for 13% -> 0% of each run, Pallas kernels for 0% -> 0%
where the time goes in v1:
time: 308 us; the launch traced here: 303 us
  Pallas kernels  241 us (78%)
  local copies, waits for them, and re-layouts  20.8 us (7%)
  matrix products  20.8 us (7%)
  other arithmetic  13.9 us (5%)
  blocking collectives  5.9 us (2%)
    pallas_call x1, Pallas kernels, spread(): pl.pallas_call(spread_kernel, out_shape=(jax.ShapeDtypeStruct((rows.shape...  115 us
    pallas_call x1, Pallas kernels, collect(): pl.pallas_call(collect_kernel, out_shape=jax.ShapeDtypeStruct((cols.shape...  69.8 us
    pallas_call x1, Pallas kernels, deliver(): pl.pallas_call(deliver_kernel, out_shape=jax.ShapeDtypeStruct((parts, ter...  56.3 us
    dot_general x1, matrix products, channel_plan(): jnp.dot(whole, weights, preferred_element_type=jnp.float32)  14.4 us
    unnamed x7, local copies, waits for them, and re-layouts  6.81 us

profile of v1, /device:TPU:10, one launch (start us, length us, event | category | flops | bytes accessed | tf_op | source)
XLA Modules:
  0.0 302.6 jit_solution(2587474057752295869)
XLA Ops:
  0.0 0.0 copy-start
  0.0 0.8 dynamic_slice.13
  0.8 1.2 fusion.1
  2.0 5.9 %psum.7 = f32[256,1]{0,1:T(1,128)S(1)} all-reduce(f32[256,1]{0,1:T(1,128)S(1)} %bitcast.47), channel_id=1, replica_groups=mesh['ctx'=8,'fsdp'=4] {'fsdp'}, use_global_device_ids=true, to_apply=%region_1.0 | all-reduce | flops 256 | bytes 2048 | tf_op jit(solution)/shard_map/psum | solution.py:384
  7.9 2.0 fusion.3.rows_ref
  9.9 4.7 %copy.18 = bf16[512,3,1024]{0,2,1:T(8,128)(2,1)} copy(bf16[512,3,1024]{2,0,1:T(8,128)(2,1)} %param.9) | data formatting | bytes 6291456 | tf_op args[2]
  14.6 3.9 %copy.19 = bf16[8,512,3,128]{1,3,2,0:T(8,128)(2,1)} copy(bf16[8,512,3,128]{1,3,0,2:T(8,128)(2,1)} %bitcast.39) | data formatting | bytes 6291456 | tf_op jit(solution)/shard_map/transpose | solution.py:388
  18.5 4.6 %copy.20.weight_ref = bf16[8,512,384]{2,1,0:T(8,128)(2,1)} copy(bf16[8,512,384]{1,2,0:T(8,128)(2,1)} %bitcast.38) | data formatting | bytes 6291456 | tf_op jit(solution)/shard_map/reshape | solution.py:389
  23.1 115.0 %shard_map.73 = (bf16[2048,4096]{1,0:T(8,128)(2,1)}, bf16[8,512,384]{2,1,0:T(8,128)(2,1)}) custom-call(bf16[256,1024]{1,0:T(8,128)(2,1)} %fusion.3.rows_ref, bf16[8,512,384]{2,1,0:T(8,128)(2,1)} %copy.20.weight_ref), custom_call_target="tpu_custom_call" | custom-call | tf_op jit(solution)/shard_map/pallas_call | solution.py:336
  138.1 14.4 %fusion = f32[2048,384]{1,0:T(8,128)} fusion(bf16[2048,4096]{1,0:T(8,128)(2,1)} %get-tuple-element.7, bf16[4096,384]{1,0:T(8,128)(2,1)} %bitcast.48), kind=kOutput, calls=%fused_computation.3 | convolution fusion | flops 6444023808 | bytes 23068672 | tf_op jit(solution)/shard_map/dot_general | solution.py:392
  152.5 0.7 dynamic-slice_bitcast_fusion.2
  153.2 4.7 %multiply_add_fusion = f32[2048,384]{1,0:T(8,128)S(1)} fusion(f32[2048,384]{1,0:T(8,128)} %fusion, f32[384]{0:T(512)S(1)} %get-tuple-element.11, f32[384]{0:T(512)S(1)} %get-tuple-element.10, f32[384]{0:T(512)S(1)} %get-tuple-element.9), kind=kLoop, calls=%fused_computation | loop fusion | flops 3932160 | bytes 6296064 | tf_op jit(solution)/shard_map/add | solution.py:30
  158.0 0.0 copy-start.1
  158.0 1.7 copy-done.1
  159.6 0.1 fusion.4
  159.7 0.2 copy.21
  160.0 0.1 copy.27
  160.1 0.1 copy.22
  160.3 0.7 constant_dynamic-slice_fusion
  161.0 0.1 rev.3
  161.1 1.4 reshape.38
  162.5 0.5 convolution_bitcast_fusion
  163.0 0.3 copy.24
  163.4 0.3 copy.30
  163.7 0.3 copy.25
  164.0 0.8 dynamic_slice.15
  164.8 2.9 fusion.5.cols_ref
  167.7 69.8 %shard_map.74 = bf16[2048,1024]{1,0:T(8,128)(2,1)} custom-call(bf16[2048,128]{1,0:T(8,128)(2,1)} %fusion.5.cols_ref), custom_call_target="tpu_custom_call" | custom-call | tf_op jit(solution)/shard_map/pallas_call | solution.py:353
  237.5 0.0 copy-done
  237.5 5.9 %convolution_convert_fusion = bf16[2048,512]{1,0:T(8,128)(2,1)} fusion(bf16[2048,1024]{1,0:T(8,128)(2,1)} %shard_map.74, bf16[1024,512]{1,0:T(8,128)(2,1)S(1)} %copy-done), kind=kOutput, calls=%fused_computation.1 | convolution fusion | flops 2148532224 | bytes 7340032 | tf_op jit(solution)/shard_map/dot_general | solution.py:413
  243.4 56.3 %shard_map.75 = bf16[4,256,1024]{2,1,0:T(8,128)(2,1)} custom-call(bf16[8,256,512]{2,1,0:T(8,128)(2,1)} %bitcast.42), custom_call_target="tpu_custom_call" | custom-call | tf_op jit(solution)/shard_map/pallas_call | solution.py:366
  299.7 2.9 reduce_sum.22
  (5 shorter events, 0.1 us)
Async XLA Ops:
  0.0 237.5 %copy-start = (bf16[1024,512]{1,0:T(8,128)(2,1)S(1)}, bf16[1024,512]{1,0:T(8,128)(2,1)}, u32[]{:S(2)}) copy-start(bf16[1024,512]{1,0:T(8,128)(2,1)} %param.13) | copy-start | bytes 3145732
  158.0 1.7 copy-start.1

commit v2 on v1

--- a/solution.py
+++ b/solution.py
@@ -82,7 +82,7 @@
 
 
 class Relay:
-    def __init__(self, own, place, sends, recvs, across):
+    def __init__(self, own, place, sends, recvs, across, half=None):
         self.me = (lax.axis_index("ctx"), lax.axis_index("fsdp"))
         self.line = lax.axis_size("ctx") // 2
         self.width = lax.axis_size("fsdp")
@@ -90,6 +90,7 @@
         self.own, self.place = own, place
         self.sends, self.recvs = sends, recvs
         self.across = across
+        self.half = half
 
     def copy(self, kind, block, target, own=False):
         index = block[0] * self.width + block[1]
@@ -117,6 +118,8 @@
         elif kind == 3:
             x, core = fsdp // 2, fsdp % 2
             action(self.copy(3, block, (ctx, (1 - x) * 2 + core), own))
+        elif self.half is not None:
+            action(self.half(block, own))
         else:
             action(self.copy(4, block, (ctx, fsdp + 1 - 2 * (fsdp % 2)), own))
 
@@ -173,10 +176,15 @@
         self.run(lambda copy: copy.wait_send(), lambda block: None)
 
 
-def spread_kernel(rows_ref, weight_ref, all_ref, mine_ref, sends, recvs, w_sends, w_recvs, local):
+def spread_kernel(
+    rows_ref, weight_ref, out_ref, all_ref, mine_ref, theirs_ref,
+    sends, recvs, w_sends, w_recvs, o_sems, local,
+):
     ctx, fsdp = lax.axis_index("ctx"), lax.axis_index("fsdp")
     slabs = lax.axis_size("ctx")
     rows, features = rows_ref.shape
+    kinds, depth, share = weight_ref.shape
+    width = share // slabs
     others = [((ctx + step) % slabs, fsdp) for step in range(1, slabs)]
     x, core = fsdp // 2, fsdp % 2
     meet(others + [(ctx, (1 - x) * 2 + core), (ctx, x * 2 + 1 - core)])
@@ -184,60 +192,99 @@
     def place(slab, part):
         return all_ref.at[pl.ds(slab * rows, rows), pl.ds(part * features, features)]
 
-    own = [
-        pltpu.make_async_copy(rows_ref, place(ctx, fsdp), local.at[0]),
-        pltpu.make_async_copy(weight_ref.at[ctx], mine_ref.at[ctx], local.at[1]),
+    def piece(kind, slab):
+        return weight_ref.at[kind, :, pl.ds(slab * width, width)]
+
+    def landing(kind, slab):
+        return mine_ref.at[pl.ds(slab * depth, depth), pl.ds(kind * width, width)]
+
+    own = [pltpu.make_async_copy(rows_ref, place(ctx, fsdp), local.at[0])] + [
+        pltpu.make_async_copy(piece(kind, ctx), landing(kind, ctx), local.at[1 + kind])
+        for kind in range(kinds)
     ]
 
-    def weight_copy(step):
-        target = (ctx + step) % slabs
-        return pltpu.make_async_remote_copy(
-            src_ref=weight_ref.at[target],
-            dst_ref=mine_ref.at[ctx],
-            send_sem=w_sends.at[step],
-            recv_sem=w_recvs.at[step],
-            device_id=(target, fsdp),
-            device_id_type=MESH,
-        )
+    def weight_copies(step, away):
+        return [
+            pltpu.make_async_remote_copy(
+                src_ref=piece(kind, away),
+                dst_ref=landing(kind, ctx),
+                send_sem=w_sends.at[step, kind],
+                recv_sem=w_recvs.at[step, kind],
+                device_id=(away, fsdp),
+                device_id_type=MESH,
+            )
+            for kind in range(kinds)
+        ]
+
+    def arrived_weights(step):
+        source = (ctx + slabs - step) % slabs
+        for kind in range(kinds):
+            pltpu.make_async_remote_copy(
+                src_ref=piece(kind, source),
+                dst_ref=landing(kind, source),
+                send_sem=w_sends.at[step, kind],
+                recv_sem=w_recvs.at[step, kind],
+                device_id=(source, fsdp),
+                device_id_type=MESH,
+            ).wait_recv()
 
     def send_weights():
         for step in range(1, slabs):
-            weight_copy(step).start()
-
+            for copy in weight_copies(step, (ctx + step) % slabs):
+                copy.start()
+
+    swap = pltpu.make_async_remote_copy(
+        src_ref=out_ref,
+        dst_ref=theirs_ref,
+        send_sem=o_sems.at[0],
+        recv_sem=o_sems.at[1],
+        device_id=(ctx, x * 2 + 1 - core),
+        device_id_type=MESH,
+    )
     relay = Relay(rows_ref, place, sends, recvs, (3, 4))
     for copy in own:
         copy.start()
+    swap.start()
     relay.go(send_weights)
     for step in range(1, slabs):
-        source = (ctx + slabs - step) % slabs
-        pltpu.make_async_remote_copy(
-            src_ref=weight_ref.at[source],
-            dst_ref=mine_ref.at[source],
-            send_sem=w_sends.at[step],
-            recv_sem=w_recvs.at[step],
-            device_id=(source, fsdp),
-            device_id_type=MESH,
-        ).wait_recv()
+        arrived_weights(step)
     relay.finish()
     for step in range(1, slabs):
-        weight_copy(step).wait_send()
+        for copy in weight_copies(step, (ctx + step) % slabs):
+            copy.wait_send()
+    swap.wait()
     for copy in own:
         copy.wait()
 
 
-def collect_kernel(cols_ref, all_ref, sends, recvs, local):
+def collect_kernel(cols_ref, all_ref, other_ref, sends, recvs, half_recvs, local):
     ctx, fsdp = lax.axis_index("ctx"), lax.axis_index("fsdp")
-    slabs = lax.axis_size("ctx")
-    width = cols_ref.shape[1]
-    meet([((ctx + step) % slabs, fsdp) for step in range(1, slabs)])
+    slabs, parts = lax.axis_size("ctx"), lax.axis_size("fsdp")
+    width = cols_ref.shape[2]
+    x, core = fsdp // 2, fsdp % 2
+    partner = (ctx, x * 2 + 1 - core)
+    meet([((ctx + step) % slabs, fsdp) for step in range(1, slabs)] + [partner])
 
     def place(slab, part):
-        return all_ref.at[:, pl.ds(slab * width, width)]
+        return all_ref.at[:, :, pl.ds(slab * width, width)]
+
+    def half(block, own):
+        cols = pl.ds(block[0] * width, width)
+        return pltpu.make_async_remote_copy(
+            src_ref=cols_ref.at[1 - core] if own else all_ref.at[1 - core, :, cols],
+            dst_ref=other_ref.at[:, cols],
+            send_sem=sends.at[3, block[0] * parts + fsdp],
+            recv_sem=half_recvs.at[block[0]],
+            device_id=partner,
+            device_id_type=MESH,
+        )
 
     own = pltpu.make_async_copy(cols_ref, place(ctx, fsdp), local.at[0])
     own.start()
-    relay = Relay(cols_ref, place, sends, recvs, ())
+    relay = Relay(cols_ref, place, sends, recvs, (4,), half)
     relay.go()
+    for step in range(slabs):
+        half(((ctx + step) % slabs, fsdp), False).wait_recv()
     relay.finish()
     own.wait()
 
@@ -247,77 +294,76 @@
     slabs, parts = lax.axis_size("ctx"), lax.axis_size("fsdp")
     fold = slabs // parts
     width = terms_ref.shape[2]
+    x, core = fsdp // 2, fsdp % 2
     home = ctx // fold
-    mixed_in = home == fsdp
+    stays = (home == fsdp) & (ctx % 2 == core)
+    targets = [(ctx // 2 + step) % (slabs // 2) for step in range(slabs // 2)]
+    sources = [(half, other) for half in range(fold) for other in range(parts // 2)]
+
+    def to_others(action):
+        for high in targets:
+            @pl.when(jnp.logical_not(stays & (high == ctx // 2)))
+            def _():
+                action(high, (high * 2 + core, home))
+
+    def from_others(action):
+        for half, other in sources:
+            source = (fsdp * fold + half, other * 2 + ctx % 2)
+
+            @pl.when(jnp.logical_not((source[0] == ctx) & (source[1] == fsdp)))
+            def _():
+                action(half, other, source)
 
     barrier = pltpu.get_barrier_semaphore()
-    for slab in range(slabs):
-        @pl.when(jnp.logical_not(mixed_in & (slab == ctx)))
-        def _():
-            pl.semaphore_signal(barrier, inc=1, device_id=(slab, home), device_id_type=MESH)
-
-    for part in range(parts):
-        for half in range(fold):
-            source = fsdp * fold + half
-
-            @pl.when(jnp.logical_not((part == fsdp) & (source == ctx)))
-            def _():
-                pl.semaphore_signal(barrier, inc=1, device_id=(source, part), device_id_type=MESH)
-
-    @pl.when(mixed_in)
+
+    def greet(device):
+        pl.semaphore_signal(barrier, inc=1, device_id=device, device_id_type=MESH)
+
+    to_others(lambda high, device: greet(device))
+    from_others(lambda half, other, device: greet(device))
+
+    @pl.when(stays)
     def _():
-        pl.semaphore_wait(barrier, slabs + parts * fold - 2)
-
-    @pl.when(jnp.logical_not(mixed_in))
+        pl.semaphore_wait(barrier, len(targets) + len(sources) - 2)
+
+    @pl.when(jnp.logical_not(stays))
     def _():
-        pl.semaphore_wait(barrier, slabs + parts * fold)
-
-    def slot(part, source):
-        return out_ref.at[part, :, pl.ds((source % fold) * width, width)]
-
-    def outgoing(slab):
+        pl.semaphore_wait(barrier, len(targets) + len(sources))
+
+    def slot(half, other):
+        return out_ref.at[other, :, pl.ds(half * width, width)]
+
+    def outgoing(high, device):
         return pltpu.make_async_remote_copy(
-            src_ref=terms_ref.at[slab],
-            dst_ref=slot(fsdp, ctx),
-            send_sem=sends.at[slab],
-            recv_sem=recvs.at[fsdp * fold + ctx % fold],
-            device_id=(slab, home),
+            src_ref=terms_ref.at[high],
+            dst_ref=slot(ctx % fold, x),
+            send_sem=sends.at[high],
+            recv_sem=recvs.at[x * fold + ctx % fold],
+            device_id=device,
             device_id_type=MESH,
         )
 
-    def each(action):
-        for step in range(slabs):
-            slab = (ctx + step) % slabs
-
-            @pl.when(jnp.logical_not(mixed_in & (slab == ctx)))
-            def _():
-                action(slab)
-
-    own = pltpu.make_async_copy(terms_ref.at[ctx], slot(fsdp, ctx), local.at[0])
-    each(lambda slab: outgoing(slab).start())
-
-    @pl.when(mixed_in)
+    def incoming(half, other, device):
+        return pltpu.make_async_remote_copy(
+            src_ref=terms_ref.at[0],
+            dst_ref=slot(half, other),
+            send_sem=sends.at[0],
+            recv_sem=recvs.at[other * fold + half],
+            device_id=device,
+            device_id_type=MESH,
+        )
+
+    own = pltpu.make_async_copy(terms_ref.at[ctx // 2], slot(ctx % fold, x), local.at[0])
+    to_others(lambda high, device: outgoing(high, device).start())
+
+    @pl.when(stays)
     def _():
         own.start()
 
-    for part in range(parts):
-        for half in range(fold):
-            source = fsdp * fold + half
-
-            @pl.when(jnp.logical_not((part == fsdp) & (source == ctx)))
-            def _():
-                pltpu.make_async_remote_copy(
-                    src_ref=terms_ref.at[0],
-                    dst_ref=slot(part, source),
-                    send_sem=sends.at[0],
-                    recv_sem=recvs.at[part * fold + half],
-                    device_id=(source, part),
-                    device_id_type=MESH,
-                ).wait_recv()
-
-    each(lambda slab: outgoing(slab).wait_send())
-
-    @pl.when(mixed_in)
+    from_others(lambda half, other, device: incoming(half, other, device).wait_recv())
+    to_others(lambda high, device: outgoing(high, device).wait_send())
+
+    @pl.when(stays)
     def _():
         own.wait()
 
@@ -331,31 +377,38 @@
     return pltpu.CompilerParams(collective_id=number, has_side_effects=True)
 
 
-def spread(rows, weights):
-    slabs, parts = lax.axis_size("ctx"), lax.axis_size("fsdp")
+def spread(rows, weights, out_weight):
+    slabs, parts = lax.axis_size("ctx"), lax.axis_size("fsdp")
+    kinds, depth, share = weights.shape
     return pl.pallas_call(
         spread_kernel,
         out_shape=(
             jax.ShapeDtypeStruct((rows.shape[0] * slabs, rows.shape[1] * parts), rows.dtype),
-            jax.ShapeDtypeStruct(weights.shape, weights.dtype),
+            jax.ShapeDtypeStruct((depth * slabs, kinds * share // slabs), weights.dtype),
+            jax.ShapeDtypeStruct(out_weight.shape, out_weight.dtype),
         ),
-        in_specs=[VMEM_SPEC, VMEM_SPEC],
-        out_specs=(ANY_SPEC, ANY_SPEC),
+        in_specs=[VMEM_SPEC, VMEM_SPEC, VMEM_SPEC],
+        out_specs=(ANY_SPEC, ANY_SPEC, ANY_SPEC),
         scratch_shapes=[
-            DMA((5, slabs * parts)), DMA((slabs * parts,)), DMA((slabs,)), DMA((slabs,)), DMA((2,)),
+            DMA((5, slabs * parts)), DMA((slabs * parts,)),
+            DMA((slabs, kinds)), DMA((slabs, kinds)), DMA((2,)), DMA((1 + kinds,)),
         ],
         compiler_params=params(0),
-    )(rows, weights)
+    )(rows, weights, out_weight)
 
 
 def collect(cols):
     slabs, parts = lax.axis_size("ctx"), lax.axis_size("fsdp")
+    halves, rows, width = cols.shape
     return pl.pallas_call(
         collect_kernel,
-        out_shape=jax.ShapeDtypeStruct((cols.shape[0], cols.shape[1] * slabs), cols.dtype),
+        out_shape=(
+            jax.ShapeDtypeStruct((halves, rows, width * slabs), cols.dtype),
+            jax.ShapeDtypeStruct((rows, width * slabs), cols.dtype),
+        ),
         in_specs=[VMEM_SPEC],
-        out_specs=ANY_SPEC,
-        scratch_shapes=[DMA((3, slabs * parts)), DMA((slabs * parts,)), DMA((1,))],
+        out_specs=(ANY_SPEC, ANY_SPEC),
+        scratch_shapes=[DMA((5, slabs * parts)), DMA((slabs * parts,)), DMA((slabs,)), DMA((1,))],
         compiler_params=params(1),
     )(cols)
 
@@ -365,10 +418,10 @@
     fold = slabs // parts
     return pl.pallas_call(
         deliver_kernel,
-        out_shape=jax.ShapeDtypeStruct((parts, terms.shape[1], terms.shape[2] * fold), terms.dtype),
+        out_shape=jax.ShapeDtypeStruct((parts // 2, terms.shape[1], terms.shape[2] * fold), terms.dtype),
         in_specs=[VMEM_SPEC],
         out_specs=ANY_SPEC,
-        scratch_shapes=[DMA((slabs,)), DMA((parts * fold,)), DMA((1,))],
+        scratch_shapes=[DMA((slabs // 2,)), DMA((fold * parts // 2,)), DMA((1,))],
         compiler_params=params(2),
     )(terms)
 
@@ -385,16 +438,15 @@
     gain = lax.dynamic_slice_in_dim(norm_gain, fsdp * features, features, 0)
     normed = (values * lax.rsqrt(mean_square + 1e-06) * gain).astype(jnp.bfloat16)
 
-    pieces = in_weight.reshape(in_weight.shape[0], 3, slabs, own).transpose(2, 0, 1, 3)
-    pieces = pieces.reshape(slabs, in_weight.shape[0], 3 * own)
-    whole, weights = spread(normed, pieces)
-    weights = weights.reshape(slabs * in_weight.shape[0], 3 * own)
-    proj = jnp.dot(whole, weights, preferred_element_type=jnp.float32).astype(jnp.bfloat16)
+    whole, weights, partner_weight = spread(normed, in_weight.transpose(1, 0, 2), out_weight)
+    proj = jnp.dot(whole, weights, preferred_element_type=jnp.float32)
+    proj = lax.reduce_precision(proj, 8, 7).astype(jnp.bfloat16)
 
     taps = lax.dynamic_slice_in_dim(short_filter, ctx * own, own, 2).reshape(3, 3 * own)
     extended = jnp.pad(proj.astype(jnp.float32), ((2, 0), (0, 0)))
     filtered = short_conv(taps, extended)
-    product = (filtered[:, own : 2 * own] * filtered[:, 2 * own :]).astype(jnp.bfloat16)
+    product = filtered[:, own : 2 * own] * filtered[:, 2 * own :]
+    product = lax.reduce_precision(product, 8, 7).astype(jnp.bfloat16)
 
     flen = long_filter.shape[1]
     group_count = long_filter.shape[0] // slabs
@@ -410,8 +462,12 @@
     skip = lax.dynamic_slice_in_dim(skip_gain, ctx * own, own, 0)
     gated = (filtered[:, :own] * (conv + skip * product.astype(jnp.float32))).astype(jnp.bfloat16)
 
-    terms = jnp.dot(collect(gated), out_weight, preferred_element_type=jnp.float32)
-    terms = terms.astype(jnp.bfloat16).reshape(slabs, rows, out_weight.shape[1])
+    by_core = gated.reshape(slabs // 2, 2, rows, own).transpose(1, 0, 2, 3)
+    every, partner_cols = collect(by_core.reshape(2, positions // 2, own))
+    core_cols = lax.dynamic_index_in_dim(every, fsdp % 2, 0, keepdims=False)
+    terms = jnp.dot(core_cols, out_weight, preferred_element_type=jnp.float32)
+    terms += jnp.dot(partner_cols, partner_weight, preferred_element_type=jnp.float32)
+    terms = terms.astype(jnp.bfloat16).reshape(slabs // 2, rows, out_weight.shape[1])
     arrived = deliver(terms)
     return jnp.sum(arrived.astype(jnp.float32), axis=0).astype(jnp.bfloat16)
 

time: 308 us -> 278 us (0.903); the launches traced: 303 us -> 277 us
  Pallas kernels: 241 us -> 220 us
  local copies, waits for them, and re-layouts: 20.8 us -> 16.6 us
    pallas_call x2, Pallas kernels: 126 us -> 105 us  [the longest x1 71.6 us: collect(): pl.pallas_call(collect_kernel, out_shape=(jax.ShapeDtypeStruct((halves, r...]
    transpose x1 -> x0, local copies, waits for them, and re-layouts: 3.86 us -> none  [channel_plan(): in_weight.reshape(in_weight.shape[0], 3, slabs, own).transpose(2, 0, 1, 3)]
    reshape x1, local copies, waits for them, and re-layouts: 4.65 us -> 0.83 us  [channel_plan(): by_core = gated.reshape(slabs // 2, 2, rows, own).transpose(1, 0, 2, 3)]
    unnamed x7 -> x10, local copies, waits for them, and re-layouts: 6.81 us -> 3.28 us
    dot_general x2 -> x3, matrix products: 20.3 us -> 19.9 us  [the longest x1 14.4 us: channel_plan(): proj = jnp.dot(whole, weights, preferred_element_type=jnp.float32)]
where the time goes in v2:
time: 278 us; the launch traced here: 277 us
  Pallas kernels  220 us (79%)
  matrix products  21.8 us (8%)
  local copies, waits for them, and re-layouts  16.6 us (6%)
  other arithmetic  13 us (5%)
  blocking collectives  5.9 us (2%)
    pallas_call x1, Pallas kernels, spread(): pl.pallas_call(spread_kernel, out_shape=(jax.ShapeDtypeStruct((rows.shape...  116 us
    pallas_call x1, Pallas kernels, collect(): pl.pallas_call(collect_kernel, out_shape=(jax.ShapeDtypeStruct((halves, r...  71.6 us
    pallas_call x1, Pallas kernels, deliver(): pl.pallas_call(deliver_kernel, out_shape=jax.ShapeDtypeStruct((parts // 2...  33 us
    dot_general x1, matrix products, channel_plan(): proj = jnp.dot(whole, weights, preferred_element_type=jnp.float32)  14.4 us
    psum x1, blocking collectives, channel_plan(): lax.psum(jnp.sum(values * values, axis=-1, keepdims=True), 'fsdp')  5.9 us

profile of v2, /device:TPU:10, one launch (start us, length us, event | category | flops | bytes accessed | tf_op | source)
XLA Modules:
  0.0 277.5 jit_solution(2553902764363136959)
XLA Ops:
  0.0 0.0 copy-start
  0.0 0.7 dynamic_slice.17
  0.7 1.2 fusion.4
  1.9 5.9 %psum.7 = f32[256,1]{0,1:T(1,128)S(1)} all-reduce(f32[256,1]{0,1:T(1,128)S(1)} %bitcast.52), channel_id=1, replica_groups=mesh['ctx'=8,'fsdp'=4] {'fsdp'}, use_global_device_ids=true, to_apply=%region_1.0 | all-reduce | flops 256 | bytes 2048 | tf_op jit(solution)/shard_map/psum | solution.py:437
  7.8 2.0 fusion.6.rows_ref
  9.9 115.6 %shard_map.73 = (bf16[2048,4096]{1,0:T(8,128)(2,1)}, bf16[4096,384]{1,0:T(8,128)(2,1)}, bf16[1024,512]{1,0:T(8,128)(2,1)}) custom-call(bf16[256,1024]{1,0:T(8,128)(2,1)} %fusion.6.rows_ref, bf16[3,512,1024]{2,1,0:T(8,128)(2,1)} %bitcast.44, bf16[1024,512]{1,0:T(8,128)(2,1)} %out_ref.1), custom_call_target="tpu_custom_call" | custom-call | tf_op jit(solution)/shard_map/pallas_call | solution.py:383
  125.5 14.4 %fusion = f32[2048,384]{1,0:T(8,128)} fusion(bf16[2048,4096]{1,0:T(8,128)(2,1)} %get-tuple-element.10, bf16[4096,384]{1,0:T(8,128)(2,1)} %get-tuple-element.11), kind=kOutput, calls=%fused_computation.2 | convolution fusion | flops 6444810240 | bytes 23068672 | tf_op jit(solution)/shard_map/dot_general | solution.py:442
  139.9 0.7 dynamic-slice_bitcast_fusion.2
  140.6 5.0 %multiply_add_fusion = f32[2048,384]{1,0:T(8,128)S(1)} fusion(f32[2048,384]{1,0:T(8,128)} %fusion, f32[384]{0:T(512)S(1)} %get-tuple-element.17, f32[384]{0:T(512)S(1)} %get-tuple-element.16, f32[384]{0:T(512)S(1)} %get-tuple-element.15), kind=kLoop, calls=%fused_computation | loop fusion | flops 3932160 | bytes 6296064 | tf_op jit(solution)/shard_map/add | solution.py:30
  145.6 0.9 fusion.8
  146.5 2.0 copy.12
  148.6 1.1 copy.19
  149.7 0.1 copy.13
  149.9 0.0 copy-start.1
  149.9 0.8 copy-done.1
  150.6 0.8 pad_slice_fusion
  151.5 0.0 copy-done
  151.5 0.1 rev.3
  151.6 0.9 slice.47
  152.5 3.4 %reshape.32 = bf16[8,128,255]{2,1,0:T(8,128)(2,1)} reshape(bf16[8,32640]{1,0:T(8,128)(2,1)} %slice.47) | data formatting | bytes 1044480 | tf_op jit(solution)/shard_map/reshape | solution.py:26
  155.8 1.9 convolution_bitcast_fusion
  157.7 0.3 copy.15
  158.0 1.3 copy.22
  159.4 2.6 copy.16
  162.0 0.8 dynamic_slice.19
  162.7 1.4 fusion.9
  164.2 0.8 copy.17
  165.0 71.6 %shard_map.74 = (bf16[2,1024,1024]{2,1,0:T(8,128)(2,1)}, bf16[1024,1024]{1,0:T(8,128)(2,1)}) custom-call(bf16[2,1024,128]{2,1,0:T(8,128)(2,1)} %bitcast.46), custom_call_target="tpu_custom_call" | custom-call | tf_op jit(solution)/shard_map/pallas_call | solution.py:403
  236.6 0.0 copy-start.2
  236.6 0.0 copy-start.3
  236.6 3.2 %fusion.1 = f32[1024,512]{1,0:T(8,128)S(1)} fusion(bf16[1024,512]{1,0:T(8,128)(2,1)} %out_ref.1, bf16[2,1024,1024]{2,1,0:T(8,128)(2,1)} %get-tuple-element.12, s32[]{:T(128)S(6)} %select_n.25), kind=kOutput, calls=%fused_computation.3 | convolution fusion | flops 1073741824 | bytes 5242884 | tf_op jit(solution)/shard_map/dot_general | solution.py:468
  239.9 0.0 copy-done.2
  239.9 0.0 copy-done.3
  239.9 2.2 add_convert_fusion
  242.1 33.0 %shard_map.75 = bf16[2,256,1024]{2,1,0:T(8,128)(2,1)} custom-call(bf16[4,256,512]{2,1,0:T(8,128)(2,1)} %bitcast.50), custom_call_target="tpu_custom_call" | custom-call | tf_op jit(solution)/shard_map/pallas_call | solution.py:419
  275.1 2.4 reduce_sum.22
  (4 shorter events, 0.1 us)
Async XLA Ops:
  0.0 151.5 %copy-start = (bf16[64,128]{1,0:T(8,128)(2,1)S(1)}, bf16[64,128]{1,0:T(8,128)(2,1)}, u32[]{:S(2)}) copy-start(bf16[64,128]{1,0:T(8,128)(2,1)} %param.11) | copy-start | bytes 49156
  149.9 0.8 copy-start.1
  236.6 3.3 %copy-start.2 = (bf16[1024,1024]{1,0:T(8,128)(2,1)S(1)}, bf16[1024,1024]{1,0:T(8,128)(2,1)}, u32[]{:S(2)}) copy-start(bf16[1024,1024]{1,0:T(8,128)(2,1)} %get-tuple-element.13) | copy-start | bytes 6291460
  236.6 3.3 %copy-start.3 = (bf16[1024,512]{1,0:T(8,128)(2,1)S(1)}, bf16[1024,512]{1,0:T(8,128)(2,1)}, u32[]{:S(2)}) copy-start(bf16[1024,512]{1,0:T(8,128)(2,1)} %get-tuple-element.14) | copy-start | bytes 3145732

commit v3 on v2

--- a/solution.py
+++ b/solution.py
@@ -146,8 +146,8 @@
                     landed(block)
                     for kind in (1, 2) + self.across:
                         self.visit(kind, block, False, action)
-            if away == 1 and after_first is not None:
-                after_first()
+            if away < self.line and after_first is not None:
+                after_first(away)
             if away >= 1:
                 back = away - 1
                 for sign in (-1, 1) if back else (1,):
@@ -203,35 +203,37 @@
         for kind in range(kinds)
     ]
 
-    def weight_copies(step, away):
+    def weight_copies(owner, source, target):
         return [
             pltpu.make_async_remote_copy(
-                src_ref=piece(kind, away),
-                dst_ref=landing(kind, ctx),
-                send_sem=w_sends.at[step, kind],
-                recv_sem=w_recvs.at[step, kind],
-                device_id=(away, fsdp),
+                src_ref=piece(kind, target),
+                dst_ref=landing(kind, source),
+                send_sem=w_sends.at[target, kind],
+                recv_sem=w_recvs.at[source, kind],
+                device_id=(owner, fsdp),
                 device_id_type=MESH,
             )
             for kind in range(kinds)
         ]
 
-    def arrived_weights(step):
-        source = (ctx + slabs - step) % slabs
-        for kind in range(kinds):
-            pltpu.make_async_remote_copy(
-                src_ref=piece(kind, source),
-                dst_ref=landing(kind, source),
-                send_sem=w_sends.at[step, kind],
-                recv_sem=w_recvs.at[step, kind],
-                device_id=(source, fsdp),
-                device_id_type=MESH,
-            ).wait_recv()
-
-    def send_weights():
-        for step in range(1, slabs):
-            for copy in weight_copies(step, (ctx + step) % slabs):
-                copy.start()
+    line, high, low = slabs // 2, ctx // 2, ctx % 2
+
+    def send_to(target):
+        for copy in weight_copies(target, ctx, target):
+            copy.start()
+
+    def send_weights(away):
+        for goal in range(line):
+            up = (high == away) & (goal > high)
+            down = (line - 1 - high == away) & (goal < high)
+
+            @pl.when(up | down)
+            def _():
+                send_to(goal * 2 + low)
+
+        if away == line - 1:
+            for step in range(line):
+                send_to((high + step) % line * 2 + 1 - low)
 
     swap = pltpu.make_async_remote_copy(
         src_ref=out_ref,
@@ -247,10 +249,13 @@
     swap.start()
     relay.go(send_weights)
     for step in range(1, slabs):
-        arrived_weights(step)
+        source = (ctx + step) % slabs
+        for copy in weight_copies(source, source, source):
+            copy.wait_recv()
     relay.finish()
     for step in range(1, slabs):
-        for copy in weight_copies(step, (ctx + step) % slabs):
+        target = (ctx + step) % slabs
+        for copy in weight_copies(target, ctx, target):
             copy.wait_send()
     swap.wait()
     for copy in own:
@@ -426,6 +431,69 @@
     )(terms)
 
 
+def mix_kernel(
+    group_width, rows_ref, weight_ref, taps_ref, base_ref, skip_ref, out_ref, bands, tail, last
+):
+    groups, window = base_ref.shape
+    flen = window // 2
+    own = out_ref.shape[2]
+
+    @pl.when(pl.program_id(0) == 0)
+    def _():
+        tail[...] = jnp.zeros_like(tail)
+        last[...] = jnp.zeros_like(last)
+        for group in range(groups):
+            row = jnp.broadcast_to(base_ref[group : group + 1, :], (flen, window))
+            band = pltpu.roll(row, 0, 1, stride=1, stride_axis=0)
+            bands[pl.ds(group * flen, flen), :] = band.astype(jnp.bfloat16)
+
+    proj = jnp.dot(rows_ref[...], weight_ref[...], preferred_element_type=jnp.float32)
+    proj = proj.astype(jnp.bfloat16).astype(jnp.float32)
+    rows = proj.shape[0]
+    ahead = tail.shape[0]
+    extended = jnp.concatenate([tail[...], proj], axis=0)
+    tail[...] = proj[rows - ahead :]
+    filtered = short_conv(
+        [taps_ref[tap : tap + 1, :] for tap in range(3)], extended[ahead - 2 :]
+    )
+    product = (filtered[:, own : 2 * own] * filtered[:, 2 * own :]).astype(jnp.bfloat16)
+    reach = jnp.concatenate([last[...], product], axis=0)
+    last[...] = product[rows - flen :]
+    lane_group = lax.broadcasted_iota(jnp.int32, (flen, own), 1) // group_width
+    for start in range(0, rows, flen):
+        every = jnp.dot(
+            bands[...], reach[start : start + window], preferred_element_type=jnp.float32
+        )
+        conv = every[:flen]
+        for group in range(1, groups):
+            conv = jnp.where(lane_group == group, every[group * flen : (group + 1) * flen], conv)
+        here = product[start : start + flen].astype(jnp.float32)
+        gate = filtered[start : start + flen, :own]
+        out_ref[0, start : start + flen, :] = (gate * (conv + skip_ref[...] * here)).astype(jnp.bfloat16)
+
+
+def mix(whole, weights, taps, base, skip, slab_rows, group_width):
+    positions, depth = whole.shape
+    own = skip.shape[1]
+    groups, window = base.shape
+    full = lambda array: pl.BlockSpec(array.shape, lambda i: (0, 0))
+    return pl.pallas_call(
+        functools.partial(mix_kernel, group_width),
+        grid=(positions // slab_rows,),
+        out_shape=jax.ShapeDtypeStruct((2, positions // 2, own), jnp.bfloat16),
+        in_specs=[
+            pl.BlockSpec((slab_rows, depth), lambda i: (i, 0)),
+            full(weights), full(taps), full(base), full(skip),
+        ],
+        out_specs=pl.BlockSpec((1, slab_rows, own), lambda i: (i % 2, i // 2, 0)),
+        scratch_shapes=[
+            pltpu.VMEM((groups * window // 2, window), jnp.bfloat16),
+            pltpu.VMEM((8, 3 * own), jnp.float32),
+            pltpu.VMEM((window // 2, own), jnp.bfloat16),
+        ],
+    )(whole, weights, taps, base, skip)
+
+
 def channel_plan(tokens, norm_gain, in_weight, short_filter, long_filter, skip_gain, out_weight):
     ctx, fsdp = lax.axis_index("ctx"), lax.axis_index("fsdp")
     slabs, parts = lax.axis_size("ctx"), lax.axis_size("fsdp")
@@ -439,31 +507,14 @@
     normed = (values * lax.rsqrt(mean_square + 1e-06) * gain).astype(jnp.bfloat16)
 
     whole, weights, partner_weight = spread(normed, in_weight.transpose(1, 0, 2), out_weight)
-    proj = jnp.dot(whole, weights, preferred_element_type=jnp.float32)
-    proj = lax.reduce_precision(proj, 8, 7).astype(jnp.bfloat16)
-
     taps = lax.dynamic_slice_in_dim(short_filter, ctx * own, own, 2).reshape(3, 3 * own)
-    extended = jnp.pad(proj.astype(jnp.float32), ((2, 0), (0, 0)))
-    filtered = short_conv(taps, extended)
-    product = filtered[:, own : 2 * own] * filtered[:, 2 * own :]
-    product = lax.reduce_precision(product, 8, 7).astype(jnp.bfloat16)
-
     flen = long_filter.shape[1]
     group_count = long_filter.shape[0] // slabs
-    group_width = own // group_count
     filters = lax.dynamic_slice_in_dim(long_filter, ctx * group_count, group_count, 0)
-    blocks = jnp.pad(toeplitz_blocks(filters, flen), ((0, 0), (0, 0), (1, 0)))
-    count = positions // flen
-    tiles = product.reshape(count, flen, group_count, group_width)
-    before = jnp.pad(tiles, ((1, 0), (0, 0), (0, 0), (0, 0)))[:-1]
-    windows = jnp.concatenate([before, tiles], axis=1)
-    conv = jnp.einsum("gts,bsgc->btgc", blocks, windows, preferred_element_type=jnp.float32)
-    conv = conv.reshape(positions, own)
-    skip = lax.dynamic_slice_in_dim(skip_gain, ctx * own, own, 0)
-    gated = (filtered[:, :own] * (conv + skip * product.astype(jnp.float32))).astype(jnp.bfloat16)
-
-    by_core = gated.reshape(slabs // 2, 2, rows, own).transpose(1, 0, 2, 3)
-    every, partner_cols = collect(by_core.reshape(2, positions // 2, own))
+    base = jnp.pad(filters[:, ::-1].astype(jnp.float32), ((0, 0), (1, flen - 1)))
+    skip = lax.dynamic_slice_in_dim(skip_gain, ctx * own, own, 0)[None]
+    gated = mix(whole, weights, taps, base, skip, rows, own // group_count)
+    every, partner_cols = collect(gated)
     core_cols = lax.dynamic_index_in_dim(every, fsdp % 2, 0, keepdims=False)
     terms = jnp.dot(core_cols, out_weight, preferred_element_type=jnp.float32)
     terms += jnp.dot(partner_cols, partner_weight, preferred_element_type=jnp.float32)

time: 278 us -> 253 us (0.910)
  matrix products: 21.8 us -> 5.22 us
  local copies, waits for them, and re-layouts: 16.6 us -> 3.34 us
  Pallas kernels: 220 us -> 231 us
  other arithmetic: 13 us -> 6.29 us
    pallas_call x0 -> x1, Pallas kernels: none -> 17.5 us  [mix(): pl.pallas_call(functools.partial(mix_kernel, group_width), grid=(position...]
    dot_general x2 -> x0, matrix products: 16.3 us -> none  [the longest x1 14.4 us: channel_plan(): proj = jnp.dot(whole, weights, preferred_element_type=jnp.float32)]
    pallas_call x1, Pallas kernels: 116 us -> 106 us  [spread(): pl.pallas_call(spread_kernel, out_shape=(jax.ShapeDtypeStruct((rows.shape...]
    reshape x4 -> x0, local copies, waits for them, and re-layouts: 6.94 us -> none  [the longest x1 3.37 us: toeplitz_blocks(): return tiled[:, :row_count * window].reshape(groups, row_count, window)]
    add x1 -> x0, other arithmetic: 5 us -> none  [short_conv(): taps[0] * extended[2:] + taps[1] * extended[1:-1] + taps[2] * extended[:-2]]
    pallas_call x1, Pallas kernels: 71.6 us -> 75.3 us  [collect(): pl.pallas_call(collect_kernel, out_shape=(jax.ShapeDtypeStruct((halves, r...]
where the time goes in v3:
time: 253 us; the launch traced here: 252 us
  Pallas kernels  231 us (91%)
  other arithmetic  6.29 us (2%)
  blocking collectives  5.9 us (2%)
  matrix products  5.22 us (2%)
  local copies, waits for them, and re-layouts  3.34 us (1%)
    pallas_call x1, Pallas kernels, spread(): pl.pallas_call(spread_kernel, out_shape=(jax.ShapeDtypeStruct((rows.shape...  106 us
    pallas_call x1, Pallas kernels, collect(): pl.pallas_call(collect_kernel, out_shape=(jax.ShapeDtypeStruct((halves, r...  75.3 us
    pallas_call x1, Pallas kernels, deliver(): pl.pallas_call(deliver_kernel, out_shape=jax.ShapeDtypeStruct((parts // 2...  32.3 us
    pallas_call x1, Pallas kernels, mix(): pl.pallas_call(functools.partial(mix_kernel, group_width), grid=(position...  17.5 us
    psum x1, blocking collectives, channel_plan(): lax.psum(jnp.sum(values * values, axis=-1, keepdims=True), 'fsdp')  5.9 us

profile of v3, /device:TPU:10, one launch (start us, length us, event | category | flops | bytes accessed | tf_op | source)
XLA Modules:
  0.0 252.1 jit_solution(16350559420008516021)
XLA Ops:
  0.0 0.0 copy-start
  0.0 1.3 dynamic-slice_bitcast_fusion.1.skip_ref
  1.3 1.2 fusion.3
  2.5 5.9 %psum.7 = f32[256,1]{0,1:T(1,128)S(1)} all-reduce(f32[256,1]{0,1:T(1,128)S(1)} %bitcast.21), channel_id=1, replica_groups=mesh['ctx'=8,'fsdp'=4] {'fsdp'}, use_global_device_ids=true, to_apply=%region_1.0 | all-reduce | flops 256 | bytes 2048 | tf_op jit(solution)/shard_map/psum | solution.py:505
  8.4 0.7 constant_dynamic-slice_fusion
  9.1 0.1 rev.3
  9.2 0.7 dynamic_slice.16
  9.9 0.0 copy-done
  9.9 0.6 copy.10
  10.5 0.7 pad_convert_fusion.base_ref
  11.1 2.0 fusion.5.rows_ref
  13.2 106.2 %shard_map.73 = (bf16[2048,4096]{1,0:T(8,128)(2,1)}, bf16[4096,384]{1,0:T(8,128)(2,1)}, bf16[1024,512]{1,0:T(8,128)(2,1)}) custom-call(bf16[256,1024]{1,0:T(8,128)(2,1)} %fusion.5.rows_ref, bf16[3,512,1024]{2,1,0:T(8,128)(2,1)} %bitcast.17, bf16[1024,512]{1,0:T(8,128)(2,1)} %out_ref.1), custom_call_target="tpu_custom_call" | custom-call | tf_op jit(solution)/shard_map/pallas_call | solution.py:388
  119.4 0.0 copy-start.1
  119.4 17.5 %shard_map.74.cols_ref = bf16[2,1024,128]{2,1,0:T(8,128)(2,1)} custom-call(bf16[2048,4096]{1,0:T(8,128)(2,1)} %get-tuple-element.10.rows_ref, bf16[4096,384]{1,0:T(8,128)(2,1)} %get-tuple-element.11.weight_ref, f32[3,384]{1,0:T(4,128)} %bitcast.19, f32[8,256]{1,0:T(8,128)} %pad_convert_fusion.base_ref, f32[1,128]{1,0:T(1,128)} %dynamic-slice_bitcast_fusion.1.skip_ref), custom_call_target="tpu_custom_call" | custom-call | tf_op jit(solution)/shard_map/pallas_call | solution.py:480
  136.9 75.3 %shard_map.75 = (bf16[2,1024,1024]{2,1,0:T(8,128)(2,1)}, bf16[1024,1024]{1,0:T(8,128)(2,1)}) custom-call(bf16[2,1024,128]{2,1,0:T(8,128)(2,1)} %shard_map.74.cols_ref), custom_call_target="tpu_custom_call" | custom-call | tf_op jit(solution)/shard_map/pallas_call | solution.py:408
  212.2 0.0 copy-done.1
  212.2 0.0 copy-start.2
  212.2 0.0 copy-start.3
  212.2 3.0 %fusion = f32[1024,512]{1,0:T(8,128)S(1)} fusion(bf16[1024,512]{1,0:T(8,128)(2,1)S(1)} %copy-done.1, bf16[2,1024,1024]{2,1,0:T(8,128)(2,1)} %get-tuple-element.12, s32[]{:T(128)S(6)} %select_n.25), kind=kOutput, calls=%fused_computation | convolution fusion | flops 1073741824 | bytes 5242884 | tf_op jit(solution)/shard_map/dot_general | solution.py:519
  215.2 0.0 copy-done.2
  215.2 0.0 copy-done.3
  215.2 2.2 add_convert_fusion
  217.4 32.3 %shard_map.76 = bf16[2,256,1024]{2,1,0:T(8,128)(2,1)} custom-call(bf16[4,256,512]{2,1,0:T(8,128)(2,1)} %bitcast.18), custom_call_target="tpu_custom_call" | custom-call | tf_op jit(solution)/shard_map/pallas_call | solution.py:424
  249.7 2.4 reduce_sum.22
  (2 shorter events, 0.0 us)
Async XLA Ops:
  0.0 9.9 %copy-start = (f32[3,3,1024]{2,1,0:T(4,128)S(1)}, f32[3,3,1024]{2,1,0:T(4,128)}, u32[]{:S(2)}) copy-start(f32[3,3,1024]{2,1,0:T(4,128)} %param.10) | copy-start | bytes 110596
  119.4 92.8 %copy-start.1 = (bf16[1024,512]{1,0:T(8,128)(2,1)S(1)}, bf16[1024,512]{1,0:T(8,128)(2,1)}, u32[]{:S(2)}) copy-start(bf16[1024,512]{1,0:T(8,128)(2,1)} %out_ref.1) | copy-start | bytes 3145732
  212.2 3.0 %copy-start.2 = (bf16[1024,1024]{1,0:T(8,128)(2,1)S(1)}, bf16[1024,1024]{1,0:T(8,128)(2,1)}, u32[]{:S(2)}) copy-start(bf16[1024,1024]{1,0:T(8,128)(2,1)} %get-tuple-element.13) | copy-start | bytes 6291460
  212.2 3.0 %copy-start.3 = (bf16[1024,512]{1,0:T(8,128)(2,1)S(1)}, bf16[1024,512]{1,0:T(8,128)(2,1)}, u32[]{:S(2)}) copy-start(bf16[1024,512]{1,0:T(8,128)(2,1)} %get-tuple-element.14) | copy-start | bytes 3145732

commit v4 on v3

--- a/solution.py
+++ b/solution.py
@@ -223,9 +223,11 @@
             copy.start()
 
     def send_weights(away):
-        for goal in range(line):
-            up = (high == away) & (goal > high)
-            down = (line - 1 - high == away) & (goal < high)
+        hold = line // 2
+        for goal in range(line if away >= hold else 0):
+            below, above = high, line - 1 - high
+            up = ((below <= away) if away == hold else (below == away)) & (goal > high)
+            down = ((above <= away) if away == hold else (above == away)) & (goal < high)
 
             @pl.when(up | down)
             def _():

time: 253 us -> 243 us (0.960)
  Pallas kernels: 231 us -> 221 us
    pallas_call x1, Pallas kernels: 75.3 us -> 69.2 us  [collect(): pl.pallas_call(collect_kernel, out_shape=(jax.ShapeDtypeStruct((halves, r...]
    pallas_call x1, Pallas kernels: 106 us -> 103 us  [spread(): pl.pallas_call(spread_kernel, out_shape=(jax.ShapeDtypeStruct((rows.shape...]
where the time goes in v4:
time: 243 us; the launch traced here: 242 us
  Pallas kernels  221 us (91%)
  other arithmetic  6.29 us (3%)
  blocking collectives  5.9 us (2%)
  matrix products  5.22 us (2%)
  local copies, waits for them, and re-layouts  3.34 us (1%)
    pallas_call x1, Pallas kernels, spread(): pl.pallas_call(spread_kernel, out_shape=(jax.ShapeDtypeStruct((rows.shape...  103 us
    pallas_call x1, Pallas kernels, collect(): pl.pallas_call(collect_kernel, out_shape=(jax.ShapeDtypeStruct((halves, r...  69.2 us
    pallas_call x1, Pallas kernels, deliver(): pl.pallas_call(deliver_kernel, out_shape=jax.ShapeDtypeStruct((parts // 2...  32.1 us
    pallas_call x1, Pallas kernels, mix(): pl.pallas_call(functools.partial(mix_kernel, group_width), grid=(position...  17.5 us
    psum x1, blocking collectives, channel_plan(): lax.psum(jnp.sum(values * values, axis=-1, keepdims=True), 'fsdp')  5.9 us

profile of v4, /device:TPU:10, one launch (start us, length us, event | category | flops | bytes accessed | tf_op | source)
XLA Modules:
  0.0 242.2 jit_solution(9669596937483527132)
XLA Ops:
  0.0 0.0 copy-start
  0.0 1.3 dynamic-slice_bitcast_fusion.1.skip_ref
  1.3 1.2 fusion.3
  2.5 5.9 %psum.7 = f32[256,1]{0,1:T(1,128)S(1)} all-reduce(f32[256,1]{0,1:T(1,128)S(1)} %bitcast.21), channel_id=1, replica_groups=mesh['ctx'=8,'fsdp'=4] {'fsdp'}, use_global_device_ids=true, to_apply=%region_1.0 | all-reduce | flops 256 | bytes 2048 | tf_op jit(solution)/shard_map/psum | solution.py:507
  8.4 0.7 constant_dynamic-slice_fusion
  9.1 0.1 rev.3
  9.2 0.7 dynamic_slice.16
  9.9 0.0 copy-done
  9.9 0.6 copy.10
  10.5 0.7 pad_convert_fusion.base_ref
  11.1 2.0 fusion.5.rows_ref
  13.2 102.7 %shard_map.73 = (bf16[2048,4096]{1,0:T(8,128)(2,1)}, bf16[4096,384]{1,0:T(8,128)(2,1)}, bf16[1024,512]{1,0:T(8,128)(2,1)}) custom-call(bf16[256,1024]{1,0:T(8,128)(2,1)} %fusion.5.rows_ref, bf16[3,512,1024]{2,1,0:T(8,128)(2,1)} %bitcast.17, bf16[1024,512]{1,0:T(8,128)(2,1)} %out_ref.1), custom_call_target="tpu_custom_call" | custom-call | tf_op jit(solution)/shard_map/pallas_call | solution.py:390
  115.8 0.0 copy-start.1
  115.9 17.5 %shard_map.74.cols_ref = bf16[2,1024,128]{2,1,0:T(8,128)(2,1)} custom-call(bf16[2048,4096]{1,0:T(8,128)(2,1)} %get-tuple-element.10.rows_ref, bf16[4096,384]{1,0:T(8,128)(2,1)} %get-tuple-element.11.weight_ref, f32[3,384]{1,0:T(4,128)} %bitcast.19, f32[8,256]{1,0:T(8,128)} %pad_convert_fusion.base_ref, f32[1,128]{1,0:T(1,128)} %dynamic-slice_bitcast_fusion.1.skip_ref), custom_call_target="tpu_custom_call" | custom-call | tf_op jit(solution)/shard_map/pallas_call | solution.py:482
  133.3 69.2 %shard_map.75 = (bf16[2,1024,1024]{2,1,0:T(8,128)(2,1)}, bf16[1024,1024]{1,0:T(8,128)(2,1)}) custom-call(bf16[2,1024,128]{2,1,0:T(8,128)(2,1)} %shard_map.74.cols_ref), custom_call_target="tpu_custom_call" | custom-call | tf_op jit(solution)/shard_map/pallas_call | solution.py:410
  202.5 0.0 copy-done.1
  202.5 0.0 copy-start.2
  202.6 0.0 copy-start.3
  202.6 3.0 %fusion = f32[1024,512]{1,0:T(8,128)S(1)} fusion(bf16[1024,512]{1,0:T(8,128)(2,1)S(1)} %copy-done.1, bf16[2,1024,1024]{2,1,0:T(8,128)(2,1)} %get-tuple-element.12, s32[]{:T(128)S(6)} %select_n.25), kind=kOutput, calls=%fused_computation | convolution fusion | flops 1073741824 | bytes 5242884 | tf_op jit(solution)/shard_map/dot_general | solution.py:521
  205.5 0.0 copy-done.2
  205.6 0.0 copy-done.3
  205.6 2.2 add_convert_fusion
  207.8 32.1 %shard_map.76 = bf16[2,256,1024]{2,1,0:T(8,128)(2,1)} custom-call(bf16[4,256,512]{2,1,0:T(8,128)(2,1)} %bitcast.18), custom_call_target="tpu_custom_call" | custom-call | tf_op jit(solution)/shard_map/pallas_call | solution.py:426
  239.9 2.4 reduce_sum.22
  (2 shorter events, 0.0 us)
Async XLA Ops:
  0.0 9.9 %copy-start = (f32[3,3,1024]{2,1,0:T(4,128)S(1)}, f32[3,3,1024]{2,1,0:T(4,128)}, u32[]{:S(2)}) copy-start(f32[3,3,1024]{2,1,0:T(4,128)} %param.10) | copy-start | bytes 110596
  115.8 86.7 %copy-start.1 = (bf16[1024,512]{1,0:T(8,128)(2,1)S(1)}, bf16[1024,512]{1,0:T(8,128)(2,1)}, u32[]{:S(2)}) copy-start(bf16[1024,512]{1,0:T(8,128)(2,1)} %out_ref.1) | copy-start | bytes 3145732
  202.5 3.0 %copy-start.2 = (bf16[1024,1024]{1,0:T(8,128)(2,1)S(1)}, bf16[1024,1024]{1,0:T(8,128)(2,1)}, u32[]{:S(2)}) copy-start(bf16[1024,1024]{1,0:T(8,128)(2,1)} %get-tuple-element.13) | copy-start | bytes 6291460
  202.6 3.0 %copy-start.3 = (bf16[1024,512]{1,0:T(8,128)(2,1)S(1)}, bf16[1024,512]{1,0:T(8,128)(2,1)}, u32[]{:S(2)}) copy-start(bf16[1024,512]{1,0:T(8,128)(2,1)} %get-tuple-element.14) | copy-start | bytes 3145732

commit v5 on v4

--- a/solution.py
+++ b/solution.py
@@ -223,7 +223,7 @@
             copy.start()
 
     def send_weights(away):
-        hold = line // 2
+        hold = line - 1
         for goal in range(line if away >= hold else 0):
             below, above = high, line - 1 - high
             up = ((below <= away) if away == hold else (below == away)) & (goal > high)

time: 243 us -> 236 us (0.971)
  Pallas kernels: 221 us -> 214 us
    pallas_call x1, Pallas kernels: 69.2 us -> 51.8 us  [collect(): pl.pallas_call(collect_kernel, out_shape=(jax.ShapeDtypeStruct((halves, r...]
    pallas_call x1, Pallas kernels: 103 us -> 112 us  [spread(): pl.pallas_call(spread_kernel, out_shape=(jax.ShapeDtypeStruct((rows.shape...]
where the time goes in v5:
time: 236 us; the launch traced here: 235 us
  Pallas kernels  214 us (91%)
  other arithmetic  6.29 us (3%)
  blocking collectives  5.9 us (2%)
  matrix products  5.22 us (2%)
  local copies, waits for them, and re-layouts  3.34 us (1%)
    pallas_call x1, Pallas kernels, spread(): pl.pallas_call(spread_kernel, out_shape=(jax.ShapeDtypeStruct((rows.shape...  112 us
    pallas_call x1, Pallas kernels, collect(): pl.pallas_call(collect_kernel, out_shape=(jax.ShapeDtypeStruct((halves, r...  51.8 us
    pallas_call x1, Pallas kernels, deliver(): pl.pallas_call(deliver_kernel, out_shape=jax.ShapeDtypeStruct((parts // 2...  32 us
    pallas_call x1, Pallas kernels, mix(): pl.pallas_call(functools.partial(mix_kernel, group_width), grid=(position...  17.5 us
    psum x1, blocking collectives, channel_plan(): lax.psum(jnp.sum(values * values, axis=-1, keepdims=True), 'fsdp')  5.9 us

profile of v5, /device:TPU:10, one launch (start us, length us, event | category | flops | bytes accessed | tf_op | source)
XLA Modules:
  0.0 234.5 jit_solution(648732610532294645)
XLA Ops:
  0.0 0.0 copy-start
  0.0 1.3 dynamic-slice_bitcast_fusion.1.skip_ref
  1.3 1.2 fusion.3
  2.5 5.9 %psum.7 = f32[256,1]{0,1:T(1,128)S(1)} all-reduce(f32[256,1]{0,1:T(1,128)S(1)} %bitcast.21), channel_id=1, replica_groups=mesh['ctx'=8,'fsdp'=4] {'fsdp'}, use_global_device_ids=true, to_apply=%region_1.0 | all-reduce | flops 256 | bytes 2048 | tf_op jit(solution)/shard_map/psum | solution.py:507
  8.4 0.7 constant_dynamic-slice_fusion
  9.1 0.1 rev.3
  9.2 0.7 dynamic_slice.16
  9.9 0.0 copy-done
  9.9 0.6 copy.10
  10.5 0.7 pad_convert_fusion.base_ref
  11.1 2.0 fusion.5.rows_ref
  13.2 112.4 %shard_map.73 = (bf16[2048,4096]{1,0:T(8,128)(2,1)}, bf16[4096,384]{1,0:T(8,128)(2,1)}, bf16[1024,512]{1,0:T(8,128)(2,1)}) custom-call(bf16[256,1024]{1,0:T(8,128)(2,1)} %fusion.5.rows_ref, bf16[3,512,1024]{2,1,0:T(8,128)(2,1)} %bitcast.17, bf16[1024,512]{1,0:T(8,128)(2,1)} %out_ref.1), custom_call_target="tpu_custom_call" | custom-call | tf_op jit(solution)/shard_map/pallas_call | solution.py:390
  125.6 0.0 copy-start.1
  125.6 17.5 %shard_map.74.cols_ref = bf16[2,1024,128]{2,1,0:T(8,128)(2,1)} custom-call(bf16[2048,4096]{1,0:T(8,128)(2,1)} %get-tuple-element.10.rows_ref, bf16[4096,384]{1,0:T(8,128)(2,1)} %get-tuple-element.11.weight_ref, f32[3,384]{1,0:T(4,128)} %bitcast.19, f32[8,256]{1,0:T(8,128)} %pad_convert_fusion.base_ref, f32[1,128]{1,0:T(1,128)} %dynamic-slice_bitcast_fusion.1.skip_ref), custom_call_target="tpu_custom_call" | custom-call | tf_op jit(solution)/shard_map/pallas_call | solution.py:482
  143.1 51.8 %shard_map.75 = (bf16[2,1024,1024]{2,1,0:T(8,128)(2,1)}, bf16[1024,1024]{1,0:T(8,128)(2,1)}) custom-call(bf16[2,1024,128]{2,1,0:T(8,128)(2,1)} %shard_map.74.cols_ref), custom_call_target="tpu_custom_call" | custom-call | tf_op jit(solution)/shard_map/pallas_call | solution.py:410
  194.9 0.0 copy-done.1
  194.9 0.0 copy-start.2
  194.9 0.0 copy-start.3
  194.9 3.0 %fusion = f32[1024,512]{1,0:T(8,128)S(1)} fusion(bf16[1024,512]{1,0:T(8,128)(2,1)S(1)} %copy-done.1, bf16[2,1024,1024]{2,1,0:T(8,128)(2,1)} %get-tuple-element.12, s32[]{:T(128)S(6)} %select_n.25), kind=kOutput, calls=%fused_computation | convolution fusion | flops 1073741824 | bytes 5242884 | tf_op jit(solution)/shard_map/dot_general | solution.py:521
  197.9 0.0 copy-done.2
  197.9 0.0 copy-done.3
  197.9 2.2 add_convert_fusion
  200.1 32.0 %shard_map.76 = bf16[2,256,1024]{2,1,0:T(8,128)(2,1)} custom-call(bf16[4,256,512]{2,1,0:T(8,128)(2,1)} %bitcast.18), custom_call_target="tpu_custom_call" | custom-call | tf_op jit(solution)/shard_map/pallas_call | solution.py:426
  232.1 2.4 %reduce_sum.22 = bf16[256,1024]{1,0:T(8,128)(2,1)} reduce(bf16[2,256,1024]{2,1,0:T(8,128)(2,1)} %shard_map.76, bf16[]{:T(256)} %constant.45.clone.1), dimensions={0}, to_apply=%region_2.3 | reduce | flops 262144 | bytes 1572866 | tf_op jit(solution)/shard_map/reduce_sum | solution.py:525
  (2 shorter events, 0.0 us)
Async XLA Ops:
  0.0 9.9 %copy-start = (f32[3,3,1024]{2,1,0:T(4,128)S(1)}, f32[3,3,1024]{2,1,0:T(4,128)}, u32[]{:S(2)}) copy-start(f32[3,3,1024]{2,1,0:T(4,128)} %param.10) | copy-start | bytes 110596
  125.6 69.3 %copy-start.1 = (bf16[1024,512]{1,0:T(8,128)(2,1)S(1)}, bf16[1024,512]{1,0:T(8,128)(2,1)}, u32[]{:S(2)}) copy-start(bf16[1024,512]{1,0:T(8,128)(2,1)} %out_ref.1) | copy-start | bytes 3145732
  194.9 3.0 %copy-start.2 = (bf16[1024,1024]{1,0:T(8,128)(2,1)S(1)}, bf16[1024,1024]{1,0:T(8,128)(2,1)}, u32[]{:S(2)}) copy-start(bf16[1024,1024]{1,0:T(8,128)(2,1)} %get-tuple-element.13) | copy-start | bytes 6291460
  194.9 3.0 %copy-start.3 = (bf16[1024,512]{1,0:T(8,128)(2,1)S(1)}, bf16[1024,512]{1,0:T(8,128)(2,1)}, u32[]{:S(2)}) copy-start(bf16[1024,512]{1,0:T(8,128)(2,1)} %get-tuple-element.14) | copy-start | bytes 3145732
